TPU v7x, 32 devices: a whole 2x2x4 slice. The times are simulated.
32 devices in a mesh: grp: 2 (over y), blk: 8 (over z, x), seq: 1, ch: 2 (over core).
Axes of the slice: x: 2, y: 2, z: 4, core: 2. Of those that a mesh axis runs over, the one named last changes fastest.
Arguments:
- alignment_activity: bfloat16 [512, 128, 64], P(('grp', 'seq'), 'blk'), parts along dimension 0, may hold values from -40 to 40
- sequence_mask: int32 [512], P('grp'), parts along dimension 0, may hold values 0 or 1
- residue_mask: int32 [256], P('grp'), parts along dimension 0, may hold values 0 or 1
- lower_weights: bfloat16 [64, 32], replicated, may hold values from -0.75 to 0.75
- upper_weights: bfloat16 [64, 32], replicated, may hold values from -0.75 to 0.75
- output_projector: bfloat16 [1024, 128], replicated, may hold values from -0.1875 to 0.1875
Outputs:
- pair_update: bfloat16 [128, 256, 128], P('ch', ('grp', 'blk'), 'seq'), parts along dimension 1
There are 2 independent parts, one for each index of `grp`. A program takes and returns all parts, laid end to end along the dimension named above; an argument that names none is the same for every part. Nothing has to cross between parts.
All inputs are finite; a program needn't handle non-finite values.
Results may differ from a plain program's by a relative error of at most 0.012.
Values may be sent and summed in bfloat16 or wider, within the bound.
A program may use at most 64 MiB of HBM per device.

v0:
```python
import math
import jax
import jax.numpy as jnp
from jax import lax
from jax.sharding import PartitionSpec as P


def shards(
    alignment_activity, sequence_mask, residue_mask, lower_weights, upper_weights, output_projector
):
    local_rows, block_rows, channel_count = alignment_activity.shape
    proj_width = lower_weights.shape[1]
    pair_width = output_projector.shape[1]
    seq_count = lax.axis_size("seq")
    core_count = lax.axis_size("ch")
    seq_place = lax.axis_index("seq")
    blk_place = lax.axis_index("blk")
    core_place = lax.axis_index("ch")
    value_entries = alignment_activity.astype(jnp.float32)
    centred = value_entries - jnp.mean(value_entries, axis=-1, keepdims=True)
    variance = jnp.mean(centred * centred, axis=-1, keepdims=True)
    normed = (centred * lax.rsqrt(variance + 1e-05)).astype(jnp.bfloat16)
    rows_valid = lax.dynamic_slice_in_dim(sequence_mask, seq_place * local_rows, local_rows).astype(
        jnp.float32
    )
    res_valid = lax.dynamic_slice_in_dim(residue_mask, blk_place * block_rows, block_rows).astype(
        jnp.float32
    )
    weight = (rows_valid[:, None] * res_valid[None, :])[:, :, None]
    left_matrix = (
        jnp.einsum("sic,cd->sid", normed, lower_weights, preferred_element_type=jnp.float32)
        * weight
    ).astype(jnp.bfloat16)
    right = (
        jnp.einsum("sic,cd->sid", normed, upper_weights, preferred_element_type=jnp.float32)
        * weight
    ).astype(jnp.bfloat16)
    right_flat = right.reshape(local_rows, block_rows * proj_width)
    table = output_projector.reshape(proj_width, proj_width, pair_width)
    out_width = pair_width // core_count
    table_used = lax.dynamic_slice_in_dim(table, core_place * out_width, out_width, 2)
    used_channels = table_used.shape[2]
    piece = lax.all_gather(right_flat, "blk", axis=1, tiled=True)
    col_count = piece.shape[1] // proj_width
    block_cols = math.gcd(col_count, 128)
    block_count = col_count // block_cols
    stacked = piece.reshape(local_rows, block_count, block_cols, proj_width).transpose(1, 0, 2, 3)

    def one_block(right_part):
        outer = jnp.einsum(
            "sic,sjd->ijcd", left_matrix, right_part, preferred_element_type=jnp.float32
        ).astype(jnp.bfloat16)
        return jnp.einsum("ijcd,cde->eij", outer, table_used, preferred_element_type=jnp.float32)

    results = lax.map(one_block, stacked)
    partial_sum = results.transpose(1, 2, 0, 3).reshape(used_channels, block_rows, col_count)
    all_cols = partial_sum.shape[2]
    quarter_cols = all_cols // seq_count
    summed = lax.psum_scatter(
        partial_sum.astype(jnp.bfloat16), "seq", scatter_dimension=2, tiled=True
    ).astype(jnp.float32)
    count = jnp.sum(sequence_mask.astype(jnp.float32))
    col_valid = lax.dynamic_slice_in_dim(
        residue_mask, seq_place * quarter_cols, quarter_cols
    ).astype(jnp.float32)
    norm = res_valid[:, None] * col_valid[None, :] * count
    return (summed / jnp.maximum(norm, 1.0)[None]).astype(jnp.bfloat16)


def solution(mesh):
    in_specs = (P(("grp", "seq"), "blk", None), P("grp"), P("grp"), P(), P(), P())
    out_specs = P("ch", ("grp", "blk"), "seq")
    return jax.shard_map(shards, mesh=mesh, in_specs=in_specs, out_specs=out_specs, check_vma=False)
```

profile of v0, /device:TPU:0, one launch (start us, length us, event | category | flops | bytes accessed | tf_op | source)
XLA Modules:
  0.0 110.0 jit_solution(18392558506096459744)
XLA Ops:
  6.5 0.0 copy-start
  6.5 0.0 all-gather.2.cloned.1.call-start
  6.5 1.2 %convert_reduce_fusion = f32[256,16]{0,1:T(8,128)S(1)} fusion(bf16[256,16,64]{0,2,1:T(8,128)(2,1)} %param.6), kind=kLoop, calls=%fused_computation.4 | loop fusion | flops 520192 | bytes 540672 | tf_op jit(solution)/shard_map/reduce_sum | solution.py:20
  7.7 1.2 %fusion.23 = f32[256,16]{0,1:T(8,128)S(1)} fusion(bf16[256,16,64]{0,2,1:T(8,128)(2,1)} %param.6, f32[256,16]{0,1:T(8,128)S(1)} %broadcast_multiply_fusion.1), kind=kLoop, calls=%fused_computation.17 | loop fusion | flops 1044480 | bytes 557056 | tf_op jit(solution)/shard_map/reduce_sum | solution.py:21
  8.9 0.7 convert_element_type.40
  9.6 0.7 dynamic-slice_convert_fusion
  10.4 0.1 add_rsqrt_fusion
  10.4 2.0 %fusion.20 = bf16[256,16,32]{0,2,1:T(8,128)(2,1)} fusion(bf16[256,16,64]{0,2,1:T(8,128)(2,1)} %param.6, f32[256,16]{0,1:T(8,128)S(1)} %get-tuple-element.13, f32[256,16]{0,1:T(8,128)S(1)} %broadcast_multiply_fusion.1, f32[256,16]{0,1:T(8,128)S(1)} %get-tuple-element.14, bf16[64,32]{0,1:T(8,128)(2,1)} %param.10), kind=kOutput, calls=%fused_computation.14 | convolution fusion | flops 18087936 | bytes 839680 | tf_op jit(solution)/shard_map/sic,cd->sid/dot_general | solution.py:35
  12.5 0.0 all-gather.2.cloned.1.call-update
  12.5 0.7 convert_element_type.48
  13.1 1.4 %convert_reduce_fusion.1 = f32[]{:T(128)} fusion(s32[256]{0:T(256)} %param.7), kind=kLoop, calls=%fused_computation.31 | loop fusion | flops 511 | bytes 1028 | tf_op jit(solution)/shard_map/reduce_sum | solution.py:62
  14.5 0.8 multiply_maximum_fusion
  15.3 49.4 %all-gather.2.cloned.1.call-done = bf16[256,4096]{0,1:T(8,128)(2,1)} async-done(((bf16[256,512]{0,1:T(8,128)(2,1)}), bf16[256,4096]{0,1:T(8,128)(2,1)}) %all-gather.2.cloned.1.call-update) | async-done | bytes 2097168 | tf_op jit(solution)/shard_map/all_gather | solution.py:43
  64.6 9.9 %fusion.25 = bf16[128,32,16,32]{3,1,2,0:T(8,128)(2,1)} fusion(bf16[256,128,32,1]{0,2,3,1:T(8,128)(2,1)} %bitcast.47, bf16[256,16,64]{0,2,1:T(8,128)(2,1)} %param.6, f32[256,16]{0,1:T(8,128)S(1)} %get-tuple-element.13, f32[256,16]{0,1:T(8,128)S(1)} %broadcast_multiply_fusion.1, f32[256,16]{0,1:T(8,128)S(1)} %get-tuple-element.14, bf16[64,32]{0,1:T(8,128)(2,1)} %param.9), kind=kOutput, calls=%fused_computation.19 | convolution fusion | flops 1091829760 | bytes 6868992 | tf_op jit(solution)/shard_map/while/body/eval_jaxpr/sic,sjd->ijcd/dot_general | solution.py:50
  74.6 24.6 %copy.9 = bf16[128,32,16,32]{0,1,3,2:T(8,128)(2,1)} copy(bf16[128,32,16,32]{3,1,2,0:T(8,128)(2,1)} %fusion.25) | data formatting | bytes 8388608 | tf_op jit(solution)/shard_map/while/body/eval_jaxpr/sic,sjd->ijcd/dot_general | solution.py:50
  99.2 0.0 copy-done
  99.2 3.1 %fusion.17 = bf16[64,16,128]{2,0,1:T(8,128)(2,1)S(1)} fusion(bf16[128,32,16,32]{0,1,3,2:T(8,128)(2,1)} %copy.9, f32[16,128]{1,0:T(8,128)S(1)} %multiply_maximum_fusion, bf16[32,32,128]{2,1,0:T(8,128)(2,1)S(1)} %bitcast.46, s32[]{:T(128)S(6)} %select_n.8), kind=kOutput, calls=%fused_computation.13 | convolution fusion | flops 268959744 | bytes 4726788 | tf_op jit(solution)/shard_map/while/body/eval_jaxpr/ijcd,cde->eij/dot_general | solution.py:53
  102.3 0.9 copy.7
  (1 shorter events, 0.0 us)
Async XLA Ops:
  6.5 92.6 %copy-start = (bf16[1024,128]{1,0:T(8,128)(2,1)S(1)}, bf16[1024,128]{1,0:T(8,128)(2,1)}, u32[]{:S(2)}) copy-start(bf16[1024,128]{1,0:T(8,128)(2,1)} %param.11) | copy-start | bytes 786436
  6.5 58.1 %all-gather.2.cloned.1.call-start = ((), (), s32[]{:S(2)}) async-start(), calls=%async_computation | async-start | bytes 2359296 | tf_op jit(solution)/shard_map/all_gather | solution.py:43
Sparse Core Ops, SparseCore 0:
  12.6 51.9 all-gather.1
where the time goes:
time: 110 us
  waiting for transfers between devices  49.4 us (45%)
  local copies, waits for them, and re-layouts  25.5 us (23%)
  matrix products  15.1 us (14%)
  between operations  13.4 us (12%)
  other arithmetic  6.66 us (6%)
    all_gather x1, waiting for transfers between devices, shards(): piece = lax.all_gather(right_flat, 'blk', axis=1, tiled=True)  49.4 us
    dot_general x1, local copies, waits for them, and re-layouts, one_block(): jnp.einsum('sic,sjd->ijcd', left_matrix, right_part, preferred_element_ty...  24.6 us
    dot_general x1, matrix products, one_block(): jnp.einsum('sic,sjd->ijcd', left_matrix, right_part, preferred_element_ty...  9.94 us
    dot_general x1, matrix products, one_block(): jnp.einsum('ijcd,cde->eij', outer, table_used, preferred_element_type=jnp...  3.13 us
  transfers between devices with their start and end apart: 1, of which 1 were waited for; matrix products, arithmetic and copies ran while one was open for 3% of the time, Pallas kernels for 0%

commit v1 on v0

--- a/solution.py
+++ b/solution.py
@@ -40,7 +40,12 @@
     out_width = pair_width // core_count
     table_used = lax.dynamic_slice_in_dim(table, core_place * out_width, out_width, 2)
     used_channels = table_used.shape[2]
-    piece = lax.all_gather(right_flat, "blk", axis=1, tiled=True)
+    ring = [right_flat]
+    for hop in range(7):
+        ring.append(lax.ppermute(ring[-1], "blk", [(dev, (dev + 1) % 8) for dev in range(8)]))
+    piece = jnp.roll(
+        jnp.concatenate(ring[::-1], axis=1), (lax.axis_index("blk") + 1) * ring[0].shape[1], axis=1
+    )
     col_count = piece.shape[1] // proj_width
     block_cols = math.gcd(col_count, 128)
     block_count = col_count // block_cols

time: 110 us -> 112 us (1.018)
  waiting for transfers between devices: 49.4 us -> 63.1 us
  between operations: 13.4 us -> 0.19 us
  starting transfers between devices: 0.01 us -> 3.01 us
  matrix products: 15.1 us -> 12.7 us
    ppermute x0 -> x7, waiting for transfers between devices: none -> 63.1 us  [shards(): lax.ppermute(ring[-1], 'blk', [(dev, (dev + 1) % 8) for dev in range(8)])]
    all_gather x1 -> x0, waiting for transfers between devices: 49.4 us -> none  [shards(): piece = lax.all_gather(right_flat, 'blk', axis=1, tiled=True)]
    ppermute x0 -> x7, starting transfers between devices: none -> 3.01 us  [shards(): lax.ppermute(ring[-1], 'blk', [(dev, (dev + 1) % 8) for dev in range(8)])]
    dot_general x1, matrix products: 9.94 us -> 8.23 us  [one_block(): jnp.einsum('sic,sjd->ijcd', left_matrix, right_part, preferred_element_ty...]
  transfers between devices with their start and end apart: 1 -> 7, of which waited for: 1 -> 7; matrix products, arithmetic and copies ran while one was open for 3% -> 2% of each run, Pallas kernels for 0% -> 0%
where the time goes in v1:
time: 112 us
  waiting for transfers between devices  63.1 us (56%)
  local copies, waits for them, and re-layouts  26.6 us (24%)
  matrix products  12.7 us (11%)
  other arithmetic  6.54 us (6%)
  starting transfers between devices  3.01 us (3%)
    ppermute x7, waiting for transfers between devices, shards(): lax.ppermute(ring[-1], 'blk', [(dev, (dev + 1) % 8) for dev in range(8)])  63.1 us
    dot_general x1, local copies, waits for them, and re-layouts, one_block(): jnp.einsum('sic,sjd->ijcd', left_matrix, right_part, preferred_element_ty...  24.6 us
    dot_general x1, matrix products, one_block(): jnp.einsum('sic,sjd->ijcd', left_matrix, right_part, preferred_element_ty...  8.23 us
    dot_general x1, matrix products, one_block(): jnp.einsum('ijcd,cde->eij', outer, table_used, preferred_element_type=jnp...  3.13 us
    ppermute x7, starting transfers between devices, shards(): lax.ppermute(ring[-1], 'blk', [(dev, (dev + 1) % 8) for dev in range(8)])  3.01 us
  transfers between devices with their start and end apart: 7, of which 7 were waited for; matrix products, arithmetic and copies ran while one was open for 2% of the time, Pallas kernels for 0%

profile of v1, /device:TPU:0, one launch (start us, length us, event | category | flops | bytes accessed | tf_op | source)
XLA Modules:
  0.0 112.0 jit_solution(7083999207629955469)
XLA Ops:
  0.0 0.0 copy-start
  0.0 1.2 %convert_reduce_fusion = f32[256,16]{0,1:T(8,128)S(1)} fusion(bf16[256,16,64]{0,2,1:T(8,128)(2,1)} %param.6), kind=kLoop, calls=%fused_computation.4 | loop fusion | flops 520192 | bytes 540672 | tf_op jit(solution)/shard_map/reduce_sum | solution.py:20
  1.2 1.2 %fusion.23 = f32[256,16]{0,1:T(8,128)S(1)} fusion(bf16[256,16,64]{0,2,1:T(8,128)(2,1)} %param.6, f32[256,16]{0,1:T(8,128)S(1)} %broadcast_multiply_fusion.1), kind=kLoop, calls=%fused_computation.17 | loop fusion | flops 1044480 | bytes 557056 | tf_op jit(solution)/shard_map/reduce_sum | solution.py:21
  2.4 0.7 convert_element_type.40
  3.1 0.7 dynamic-slice_convert_fusion
  3.8 0.1 add_rsqrt_fusion
  3.9 1.3 %fusion.20 = bf16[256,16,32]{0,2,1:T(8,128)(2,1)S(1)} fusion(bf16[256,16,64]{0,2,1:T(8,128)(2,1)} %param.6, f32[256,16]{0,1:T(8,128)S(1)} %get-tuple-element.13, f32[256,16]{0,1:T(8,128)S(1)} %broadcast_multiply_fusion.1, f32[256,16]{0,1:T(8,128)S(1)} %get-tuple-element.14, bf16[64,32]{0,1:T(8,128)(2,1)} %param.10), kind=kOutput, calls=%fused_computation.14 | convolution fusion | flops 18087936 | bytes 839680 | tf_op jit(solution)/shard_map/sic,cd->sid/dot_general | solution.py:35
  5.2 3.0 %collective-permute-start = (bf16[256,512]{0,1:T(8,128)(2,1)S(1)}, bf16[256,512]{0,1:T(8,128)(2,1)S(1)}, u32[]{:S(2)}, u32[]{:S(2)}) collective-permute-start(bf16[256,512]{0,1:T(8,128)(2,1)S(1)} %bitcast.48), channel_id=1, source_target_pairs={{0,2},{2,4},{4,6},{6,8},{8,10},{10,12},{12,14},{14,0},{1,3},{3,5},... | collective-permute-start | bytes 786440 | tf_op jit(solution)/shard_map/ppermute | solution.py:45
  8.2 9.3 %collective-permute-done = bf16[256,512]{0,1:T(8,128)(2,1)S(1)} collective-permute-done((bf16[256,512]{0,1:T(8,128)(2,1)S(1)}, bf16[256,512]{0,1:T(8,128)(2,1)S(1)}, u32[]{:S(2)}, u32[]{:S(2)}) %collective-permute-start) | collective-permute-done | bytes 262176 | tf_op jit(solution)/shard_map/ppermute | solution.py:45
  17.6 0.0 collective-permute-start.1
  17.6 10.2 %collective-permute-done.1 = bf16[256,512]{0,1:T(8,128)(2,1)S(1)} collective-permute-done((bf16[256,512]{0,1:T(8,128)(2,1)S(1)}, bf16[256,512]{0,1:T(8,128)(2,1)S(1)}, u32[]{:S(2)}, u32[]{:S(2)}) %collective-permute-start.1) | collective-permute-done | bytes 262176 | tf_op jit(solution)/shard_map/ppermute | solution.py:45
  27.8 0.0 collective-permute-start.2
  27.8 9.3 %collective-permute-done.2 = bf16[256,512]{0,1:T(8,128)(2,1)S(1)} collective-permute-done((bf16[256,512]{0,1:T(8,128)(2,1)S(1)}, bf16[256,512]{0,1:T(8,128)(2,1)S(1)}, u32[]{:S(2)}, u32[]{:S(2)}) %collective-permute-start.2) | collective-permute-done | bytes 262176 | tf_op jit(solution)/shard_map/ppermute | solution.py:45
  37.0 0.0 collective-permute-start.3
  37.0 9.1 %collective-permute-done.3 = bf16[256,512]{0,1:T(8,128)(2,1)S(1)} collective-permute-done((bf16[256,512]{0,1:T(8,128)(2,1)S(1)}, bf16[256,512]{0,1:T(8,128)(2,1)S(1)}, u32[]{:S(2)}, u32[]{:S(2)}) %collective-permute-start.3) | collective-permute-done | bytes 262176 | tf_op jit(solution)/shard_map/ppermute | solution.py:45
  46.1 0.0 collective-permute-start.4
  46.1 9.1 %collective-permute-done.4 = bf16[256,512]{0,1:T(8,128)(2,1)S(1)} collective-permute-done((bf16[256,512]{0,1:T(8,128)(2,1)S(1)}, bf16[256,512]{0,1:T(8,128)(2,1)S(1)}, u32[]{:S(2)}, u32[]{:S(2)}) %collective-permute-start.4) | collective-permute-done | bytes 262176 | tf_op jit(solution)/shard_map/ppermute | solution.py:45
  55.2 0.0 collective-permute-start.5
  55.2 9.7 %collective-permute-done.5 = bf16[256,512]{0,1:T(8,128)(2,1)S(1)} collective-permute-done((bf16[256,512]{0,1:T(8,128)(2,1)S(1)}, bf16[256,512]{0,1:T(8,128)(2,1)S(1)}, u32[]{:S(2)}, u32[]{:S(2)}) %collective-permute-start.5) | collective-permute-done | bytes 262176 | tf_op jit(solution)/shard_map/ppermute | solution.py:45
  64.9 0.0 collective-permute-start.6
  64.9 1.3 %convert_reduce_fusion.1 = f32[]{:T(128)} fusion(s32[256]{0:T(256)} %param.7), kind=kLoop, calls=%fused_computation.48 | loop fusion | flops 511 | bytes 1028 | tf_op jit(solution)/shard_map/reduce_sum | solution.py:67
  66.2 0.7 convert_element_type.48
  66.8 0.7 multiply_maximum_fusion
  67.5 6.4 %collective-permute-done.6 = bf16[256,512]{0,1:T(8,128)(2,1)S(1)} collective-permute-done((bf16[256,512]{0,1:T(8,128)(2,1)S(1)}, bf16[256,512]{0,1:T(8,128)(2,1)S(1)}, u32[]{:S(2)}, u32[]{:S(2)}) %collective-permute-start.6) | collective-permute-done | bytes 262176 | tf_op jit(solution)/shard_map/ppermute | solution.py:45
  74.2 0.0 copy-start.1
  74.2 0.0 copy-start.2
  74.4 0.1 constant_dynamic-slice_fusion
  74.6 0.6 copy-done.1
  75.2 8.2 %fusion.25 = bf16[128,32,16,32]{3,1,2,0:T(8,128)(2,1)} fusion(bf16[256,128,32,1]{0,2,3,1:T(8,128)(2,1)S(1)} %bitcast.47, bf16[256,16,64]{0,2,1:T(8,128)(2,1)S(1)} %copy-done.1, f32[256,16]{0,1:T(8,128)S(1)} %get-tuple-element.13, f32[256,16]{0,1:T(8,128)S(1)} %broadcast_multiply_fusion.1, f32[256,16]{0,1:T(8,128)S(1)} %get-tuple-element.14, ...), kind=kOutput, calls=%fused_computation.19 | convolution fusion | flops 1091829760 | bytes 6868992 | tf_op jit(solution)/shard_map/while/body/eval_jaxpr/sic,sjd->ijcd/dot_general | solution.py:55
  83.4 24.6 %copy.9 = bf16[128,32,16,32]{0,1,3,2:T(8,128)(2,1)} copy(bf16[128,32,16,32]{3,1,2,0:T(8,128)(2,1)} %fusion.25) | data formatting | bytes 8388608 | tf_op jit(solution)/shard_map/while/body/eval_jaxpr/sic,sjd->ijcd/dot_general | solution.py:55
  108.0 3.1 %fusion.17 = bf16[64,16,128]{2,0,1:T(8,128)(2,1)S(1)} fusion(bf16[128,32,16,32]{0,1,3,2:T(8,128)(2,1)} %copy.9, f32[16,128]{1,0:T(8,128)S(1)} %multiply_maximum_fusion, bf16[32,32,128]{2,1,0:T(8,128)(2,1)S(1)} %bitcast.46, s32[]{:T(128)S(6)} %select_n.21), kind=kOutput, calls=%fused_computation.13 | convolution fusion | flops 268959744 | bytes 4726788 | tf_op jit(solution)/shard_map/while/body/eval_jaxpr/ijcd,cde->eij/dot_general | solution.py:58
  111.1 0.9 copy.7
  (19 shorter events, 0.3 us)
Async XLA Ops:
  0.0 108.0 %copy-start = (bf16[1024,128]{1,0:T(8,128)(2,1)S(1)}, bf16[1024,128]{1,0:T(8,128)(2,1)}, u32[]{:S(2)}) copy-start(bf16[1024,128]{1,0:T(8,128)(2,1)} %param.11) | copy-start | bytes 786436
  5.2 12.3 %collective-permute-start = (bf16[256,512]{0,1:T(8,128)(2,1)S(1)}, bf16[256,512]{0,1:T(8,128)(2,1)S(1)}, u32[]{:S(2)}, u32[]{:S(2)}) collective-permute-start(bf16[256,512]{0,1:T(8,128)(2,1)S(1)} %bitcast.48), channel_id=1, source_target_pairs={{0,2},{2,4},{4,6},{6,8},{8,10},{10,12},{12,14},{14,0},{1,3},{3,5},... | collective-permute-start | bytes 786440 | tf_op jit(solution)/shard_map/ppermute | solution.py:45
  17.6 10.2 %collective-permute-start.1 = (bf16[256,512]{0,1:T(8,128)(2,1)S(1)}, bf16[256,512]{0,1:T(8,128)(2,1)S(1)}, u32[]{:S(2)}, u32[]{:S(2)}) collective-permute-start(bf16[256,512]{0,1:T(8,128)(2,1)S(1)} %collective-permute-done), channel_id=1, source_target_pairs={{0,2},{2,4},{4,6},{6,8},{8,10},{10,12},{12,14},{14,0},{1,3},{3,5},... | collective-permute-start | bytes 786440 | tf_op jit(solution)/shard_map/ppermute | solution.py:45
  27.8 9.3 %collective-permute-start.2 = (bf16[256,512]{0,1:T(8,128)(2,1)S(1)}, bf16[256,512]{0,1:T(8,128)(2,1)S(1)}, u32[]{:S(2)}, u32[]{:S(2)}) collective-permute-start(bf16[256,512]{0,1:T(8,128)(2,1)S(1)} %collective-permute-done.1), channel_id=1, source_target_pairs={{0,2},{2,4},{4,6},{6,8},{8,10},{10,12},{12,14},{14,0},{1,3},{3,5},... | collective-permute-start | bytes 786440 | tf_op jit(solution)/shard_map/ppermute | solution.py:45
  37.0 9.1 %collective-permute-start.3 = (bf16[256,512]{0,1:T(8,128)(2,1)S(1)}, bf16[256,512]{0,1:T(8,128)(2,1)S(1)}, u32[]{:S(2)}, u32[]{:S(2)}) collective-permute-start(bf16[256,512]{0,1:T(8,128)(2,1)S(1)} %collective-permute-done.2), channel_id=1, source_target_pairs={{0,2},{2,4},{4,6},{6,8},{8,10},{10,12},{12,14},{14,0},{1,3},{3,5},... | collective-permute-start | bytes 786440 | tf_op jit(solution)/shard_map/ppermute | solution.py:45
  46.1 9.1 %collective-permute-start.4 = (bf16[256,512]{0,1:T(8,128)(2,1)S(1)}, bf16[256,512]{0,1:T(8,128)(2,1)S(1)}, u32[]{:S(2)}, u32[]{:S(2)}) collective-permute-start(bf16[256,512]{0,1:T(8,128)(2,1)S(1)} %collective-permute-done.3), channel_id=1, source_target_pairs={{0,2},{2,4},{4,6},{6,8},{8,10},{10,12},{12,14},{14,0},{1,3},{3,5},... | collective-permute-start | bytes 786440 | tf_op jit(solution)/shard_map/ppermute | solution.py:45
  55.2 9.7 %collective-permute-start.5 = (bf16[256,512]{0,1:T(8,128)(2,1)S(1)}, bf16[256,512]{0,1:T(8,128)(2,1)S(1)}, u32[]{:S(2)}, u32[]{:S(2)}) collective-permute-start(bf16[256,512]{0,1:T(8,128)(2,1)S(1)} %collective-permute-done.4), channel_id=1, source_target_pairs={{0,2},{2,4},{4,6},{6,8},{8,10},{10,12},{12,14},{14,0},{1,3},{3,5},... | collective-permute-start | bytes 786440 | tf_op jit(solution)/shard_map/ppermute | solution.py:45
  64.9 9.1 %collective-permute-start.6 = (bf16[256,512]{0,1:T(8,128)(2,1)S(1)}, bf16[256,512]{0,1:T(8,128)(2,1)S(1)}, u32[]{:S(2)}, u32[]{:S(2)}) collective-permute-start(bf16[256,512]{0,1:T(8,128)(2,1)S(1)} %collective-permute-done.5), channel_id=1, source_target_pairs={{0,2},{2,4},{4,6},{6,8},{8,10},{10,12},{12,14},{14,0},{1,3},{3,5},... | collective-permute-start | bytes 786440 | tf_op jit(solution)/shard_map/ppermute | solution.py:45
  74.2 1.0 copy-start.1
  74.2 1.0 copy-start.2
